TPU v7x, 32 devices: a whole 2x2x4 slice. The times are simulated.
32 devices in a mesh: space: 4 (over y, core), mode: 8 (over z, x).
Axes of the slice: x: 2, y: 2, z: 4, core: 2. Of those that a mesh axis runs over, the one named last changes fastest.
Arguments:
- intensity: float32 [1024, 8, 64, 256], P('mode', None, 'space'), may hold values from 0.1 to 2
- dir_cos: float32 [3, 32], replicated, may hold values from -1 to 1, as said below
- velocity: float32 [32], replicated, may hold values from 0.2 to 1
- rate: float32 [32], replicated, may hold values from 0.05 to 2
- spectrum: float32 [32], replicated, may hold values from 0.2 to 2
- weight: float32 [32], replicated, may hold values from 0.25 to 1.75
- heat: float32 [64, 256], P('space'), may hold values from 0.5 to 4
- rough_cells: int32 [4096], P('space'), may hold values from 0 to 4095, as said below
- rough_count: int32 [4], P('space'), may hold values from 256 to 1024, as said below
- rough_map: int32 [4096, 16], P('space'), may hold values from 0 to 15
Outputs:
- intensity_new: float32 [1024, 8, 64, 256], P('mode', None, 'space')
- energy_new: float32 [8, 64, 256], P(None, 'space')
Inputs may be any that keep to these rules, and one draw needn't show every extreme that they name: `dir_cos`: even directions have a positive third cosine, and direction 2k+1 equals direction 2k with the third cosine negated; every direction has a third cosine of magnitude 0.3 or more. `rough_cells`: the entries of one index of space are distinct. `rough_count`: some index of space has all 1024 slots live.
All inputs are finite; a program needn't handle non-finite values.
Results may differ from a plain program's by a relative error of at most 0.0015.
Values sent between devices are 32-bit elements; how exact they have to be, the bound alone decides.
A program may use at most 128 MiB of HBM per device.

v0:
```python
import jax
import jax.numpy as jnp
from jax import lax
from jax.sharding import PartitionSpec as P

PAIRS = 1024


def extended(block, sides, width):
    for axis, dim in sides:
        count = lax.axis_size(axis)
        forward = [(i, i + 1) for i in range(count - 1)]
        backward = [(target, source) for source, target in forward]
        low = lax.ppermute(
            lax.slice_in_dim(block, block.shape[dim] - width, None, axis=dim), axis, forward
        )
        high = lax.ppermute(lax.slice_in_dim(block, 0, width, axis=dim), axis, backward)
        block = jnp.concatenate([low, block, high], axis=dim)
    return block


def squash(energy):
    return energy / (1.0 + 0.3 * jnp.abs(energy))


def per_device(
    intensity, dir_cos, velocity, rate, spectrum, weight, heat, rough_cells, rough_count, rough_map
):
    pairs_local = intensity.shape[0]
    modes = velocity.shape[0]
    planes_count, rows, width = (intensity.shape[1], intensity.shape[2], intensity.shape[3])
    dirs_local = pairs_local // modes
    half = dirs_local // 2
    position = lax.axis_index("mode")
    cos_local = lax.dynamic_slice_in_dim(dir_cos, position * dirs_local, dirs_local, 1)
    weight_local = lax.dynamic_slice_in_dim(weight, position * dirs_local, dirs_local, 0)
    field = intensity.reshape(dirs_local, modes, planes_count, rows, width)
    partial_value = jnp.einsum("s,smzxy->zxy", weight_local, field)
    energy = lax.psum(partial_value, "mode") / PAIRS
    equil = squash(energy)
    padded = extended(field, (("space", 3),), 1)
    ox = cos_local[0][:, None, None, None, None]
    oy = cos_local[1][:, None, None, None, None]
    speed = velocity[None, :, None, None, None]
    pady = jnp.pad(field, ((0, 0), (0, 0), (0, 0), (0, 0), (1, 1)))
    along = jnp.maximum(ox, 0.0) * (field - padded[:, :, :, :-2]) + jnp.minimum(ox, 0.0) * (
        padded[:, :, :, 2:] - field
    )
    across = jnp.maximum(oy, 0.0) * (field - pady[..., :-2]) + jnp.minimum(oy, 0.0) * (
        pady[..., 2:] - field
    )
    source = (rate * spectrum)[:, None, None, None] * equil[None]
    rhs = field + source[None] - speed * (along + across)
    diag = 1.0 + rate
    couple = velocity[None, :] * jnp.abs(cos_local[2])[:, None]
    cdown = couple[1::2][:, :, None, None]
    adown = diag[None, :, None, None] + cdown
    down_rhs = rhs[1::2]
    carry = spectrum[None, :, None, None] * heat[None, None]
    planes = [None] * planes_count
    for level in reversed(range(planes_count)):
        carry = (down_rhs[:, :, level] + cdown * carry) / adown
        planes[level] = carry
    down_new = jnp.stack(planes, axis=2)
    bottom = down_new[:, :, 0].reshape(half, modes, rows * width)
    slots = rough_cells.shape[0]
    live = jnp.arange(slots, dtype=jnp.int32) < rough_count[0]
    everything = lax.all_gather(bottom, "mode", axis=0, tiled=True)
    values = everything[:, :, rough_cells]
    targets = lax.dynamic_slice_in_dim(rough_map, position * half, half, 1)
    picked = jnp.take_along_axis(values.transpose(2, 0, 1), targets[:, :, None], axis=1).transpose(
        1, 2, 0
    )
    current = bottom[:, :, rough_cells]
    inflow = 0.9 * bottom.at[:, :, rough_cells].set(jnp.where(live[None, None, :], picked, current))
    carry = inflow.reshape(half, modes, rows, width)
    cup = couple[0::2][:, :, None, None]
    aup = diag[None, :, None, None] + cup
    up_rhs = rhs[0::2]
    planes = []
    for level in range(planes_count):
        carry = (up_rhs[:, :, level] + cup * carry) / aup
        planes.append(carry)
    up_new = jnp.stack(planes, axis=2)
    fresh = jnp.stack([up_new, down_new], axis=1).reshape(
        dirs_local, modes, planes_count, rows, width
    )
    energy_new = lax.psum(jnp.einsum("s,smzxy->zxy", weight_local, fresh), "mode") / PAIRS
    return (fresh.reshape(pairs_local, planes_count, rows, width), energy_new)


def solution(mesh):
    in_specs = (
        P("mode", None, "space", None),
        P(),
        P(),
        P(),
        P(),
        P(),
        P("space", None),
        P("space"),
        P("space"),
        P("space", None),
    )
    out_specs = (P("mode", None, "space", None), P(None, "space", None))
    return jax.shard_map(
        per_device, mesh=mesh, in_specs=in_specs, out_specs=out_specs, check_vma=False
    )
```

profile of v0, /device:TPU:0, one launch (start us, length us, event | category | flops | bytes accessed | tf_op | source)
XLA Modules:
  0.0 554.9 jit_solution(16689023233069573652)
XLA Ops:
  7.2 7.9 %bitcast_reduce_fusion = bf16[4,8,16,256]{3,2,1,0:T(8,128)(2,1)S(1)} fusion(f32[128,8,16,256]{3,2,1,0:T(8,128)} %param.10), kind=kLoop, calls=%fused_computation.96 | loop fusion | flops 4063232 | bytes 17039360 | tf_op jit(solution)/shard_map/s,smzxy->zxy/reduce_sum | solution.py:38
  15.2 0.4 fusion.23
  15.5 0.7 copy.266
  16.3 8.0 %fusion.37 = (f32[4,32,8,1,256]{4,3,2,1,0:T(1,128)S(1)}, f32[4,32,8,1,256]{4,3,2,1,0:T(1,128)S(1)}) fusion(f32[4,32,8,16,256]{4,3,2,1,0:T(8,128)} %bitcast.67), kind=kLoop, calls=%fused_computation.99 | loop fusion | bytes 4194304 | tf_op jit(solution)/shard_map/slice | solution.py:15
  24.4 2.5 collective-permute-start
  26.9 1.0 copy.238
  27.9 1.5 collective-permute-start.1
  29.4 0.1 constant_dynamic-slice_fusion
  29.5 0.1 broadcast_multiply_fusion.5
  29.6 0.9 broadcast_multiply_fusion.3
  30.5 0.1 broadcast_multiply_fusion.2
  30.6 59.0 %all-reduce.4.cloned.1.call-done = f32[8,16,256]{2,1,0:T(8,128)} async-done(((f32[8,16,256]{2,1,0:T(8,128)}), f32[8,16,256]{2,1,0:T(8,128)}) %all-reduce.4.cloned.1.call-update) | async-done | bytes 131088 | tf_op jit(solution)/shard_map/psum | solution.py:39
  89.6 0.9 add_divide_fusion.8
  90.5 0.6 broadcast_multiply_fusion.1
  91.2 1.1 copy.237
  92.3 2.3 copy.239
  94.6 34.3 %fusion.5 = f32[4,32,8,16,256]{4,3,2,1,0:T(8,128)} fusion(f32[4,32,8,16,256]{4,3,2,1,0:T(8,128)} %bitcast.68, f32[4,32,8,1,256]{4,3,2,1,0:T(1,128)S(1)} %copy.239, f32[4,32,8,1,256]{4,3,2,1,0:T(1,128)S(1)} %copy.237, f32[4]{0:T(128)S(1)} %get-tuple-element.31, f32[4]{0:T(128)S(1)} %get-tuple-element.33, f32[4]{0:T(128)S(1)} %get-tuple-element.30, ...), kind=kLoop, calls=%fused_computation.11 | loop fusion | flops 67108864 | bytes 39846080 | tf_op jit(solution)/shard_map/sub | solution.py:53
  128.9 9.2 %fusion.36 = (f32[2,32,8,16,256]{4,3,2,1,0:T(8,128)}, f32[2,32,8,16,256]{4,3,2,1,0:T(8,128)S(1)}) fusion(f32[4,32,8,16,256]{4,3,2,1,0:T(8,128)} %fusion.5), kind=kLoop, calls=%fused_computation.98 | loop fusion | bytes 33554432 | tf_op jit(solution)/shard_map/slice | solution.py:79
  138.1 1.1 divide_dynamic-update-slice_fusion
  139.2 0.2 constant_dynamic-update-slice_fusion.12
  139.5 0.2 constant_dynamic-update-slice_fusion.10
  139.8 0.2 constant_dynamic-update-slice_fusion.8
  140.1 3.0 fusion.38
  143.2 3.4 copy-done.2
  146.6 2.5 squeeze.36
  149.0 2.4 squeeze.37
  151.4 2.4 squeeze.38
  153.8 2.4 squeeze.39
  156.2 2.4 squeeze.40
  158.6 1.1 squeeze.41
  159.8 0.2 squeeze.42
  160.0 0.2 squeeze.43
  160.2 4.9 add_divide_fusion.7
  165.0 0.3 all-reduce.6.cloned.1.call-start
  165.3 0.8 bitcast_or_fusion
  166.1 0.2 copy.242
  166.3 0.3 reshape.137
  166.6 0.8 and_bitcast_fusion
  167.4 0.3 copy.240
  168.4 5.9 %copy.244 = f32[2,32,4096]{1,0,2:T(2,128)} copy(f32[2,32,4096]{2,1,0:T(8,128)} %add_divide_fusion.7) | data formatting | bytes 2097152 | tf_op jit(solution)/shard_map/div | solution.py:62
  174.3 5.7 %gather_fusion.1 = f32[1024,2,32]{2,1,0:T(2,128)S(1)} fusion(f32[2,32,4096]{1,0,2:T(2,128)} %copy.244, s32[1024]{0:T(1024)S(1)} %get-tuple-element.27), kind=kCustom, calls=%fused_computation.1 | custom fusion | bytes 528384 | tf_op jit(solution)/shard_map/gather | solution.py:74
  180.0 108.7 %all-gather.2.cloned.1.call-done = f32[16,32,4096]{2,1,0:T(8,128)} async-done(((f32[2,32,4096]{2,1,0:T(8,128)}), f32[16,32,4096]{2,1,0:T(8,128)}) %all-gather.2.cloned.1.call-update) | async-done | bytes 8388624 | tf_op jit(solution)/shard_map/all_gather | solution.py:68
  288.8 23.2 %copy.241 = f32[16,32,4096]{1,0,2:T(8,128)} copy(f32[16,32,4096]{2,1,0:T(8,128)} %all-gather.2.cloned.1.call-done) | data formatting | bytes 16777216 | tf_op jit(solution)/shard_map/all_gather | solution.py:68
  312.0 19.9 %gather_fusion = f32[1024,16,32]{2,1,0:T(8,128)} fusion(f32[16,32,4096]{1,0,2:T(8,128)} %copy.241, s32[1024]{0:T(1024)S(1)} %get-tuple-element.27), kind=kCustom, calls=%fused_computation | custom fusion | bytes 4198400 | tf_op jit(solution)/shard_map/gather | solution.py:69
  331.9 20.6 %gather_fusion.2 = f32[2048,32]{1,0:T(8,128)S(1)} fusion(f32[1024,16,32]{2,1,0:T(8,128)} %gather_fusion, s32[2048]{0:T(1024)S(1)} %reshape.137), kind=kCustom, calls=%fused_computation.2 | custom fusion | bytes 540672 | tf_op jit(solution)/shard_map/jit(take_along_axis)/gather | solution.py:71
  352.5 3.9 fusion.22
  356.4 93.8 %scatter_fusion = f32[2,32,4096]{1,0,2:T(2,128)} fusion(f32[2,32,4096]{1,0,2:T(2,128)} %copy.244, s32[1024]{0:T(1024)S(1)} %get-tuple-element.28, f32[1024,2,32]{2,1,0:T(2,128)S(1)} %fusion.22), kind=kCustom, calls=%fused_computation.3 | custom fusion | bytes 790528 | tf_op jit(solution)/shard_map/scatter | solution.py:75
  450.2 5.8 %broadcast_multiply_fusion = f32[2,32,4096]{1,0,2:T(2,128)} fusion(f32[2,32,4096]{1,0,2:T(2,128)} %scatter_fusion), kind=kLoop, calls=%fused_computation.22 | loop fusion | flops 262144 | bytes 2097152 | tf_op jit(solution)/shard_map/mul | solution.py:75
  456.0 3.6 copy.254
  459.6 1.6 constant_dynamic-update-slice_fusion.6
  461.3 1.9 constant_dynamic-update-slice_fusion.5
  463.2 1.6 constant_dynamic-update-slice_fusion.4
  464.8 1.9 constant_dynamic-update-slice_fusion.3
  466.7 0.2 constant_dynamic-update-slice_fusion.2
  467.0 0.3 constant_dynamic-update-slice_fusion.1
  467.3 0.2 constant_dynamic-update-slice_fusion
  467.5 0.3 fusion.14
  467.8 1.1 slice-done.2
  468.9 1.3 slice-done.3
  470.2 6.9 %fusion.32 = (bf16[2,2,8,16,256]{4,3,2,1,0:T(8,128)(2,1)S(1)}, f32[2,2,32,8,16,256]{5,4,3,2,1,0:T(8,128)}) fusion(f32[2,1,32,8,16,256]{5,4,3,2,1,0:T(8,128)S(1)} %bitcast.76, f32[2,1,32,8,16,256]{5,4,3,2,1,0:T(8,128)S(1)} %bitcast.73), kind=kLoop, calls=%fused_computation.97 | loop fusion | flops 8257536 | bytes 33816576 | tf_op jit(solution)/shard_map/s,smzxy->zxy/reduce_sum | solution.py:88
  477.1 0.4 fusion.25
  477.5 0.7 copy.265
  478.1 68.6 %all-reduce.6.cloned.1.call-done = f32[8,16,256]{2,1,0:T(8,128)} async-done(((f32[8,16,256]{2,1,0:T(8,128)}), f32[8,16,256]{2,1,0:T(8,128)}) %all-reduce.6.cloned.1.call-update) | async-done | bytes 131088 | tf_op jit(solution)/shard_map/psum | solution.py:88
  546.8 1.6 broadcast_multiply_fusion.4
  (46 shorter events, 0.6 us)
Async XLA Ops:
  7.2 22.2 %copy-start = (f32[3,32]{1,0:T(4,128)S(1)}, f32[3,32]{1,0:T(4,128)}, u32[]{:S(2)}) copy-start(f32[3,32]{1,0:T(4,128)} %param.11) | copy-start | bytes 1156
  7.2 82.4 %all-reduce.4.cloned.1.call-start = ((), (), s32[]{:S(2)}) async-start(), calls=%async_computation | async-start | bytes 262144 | tf_op jit(solution)/shard_map/psum | solution.py:39
  7.2 7.9 %copy-start.9 = (f32[32]{0:T(128)S(1)}, f32[32]{0:T(128)}, u32[]{:S(2)}) copy-start(f32[32]{0:T(128)} %param.15) | copy-start | bytes 388
  15.1 14.4 %copy-start.4 = (f32[16,256]{1,0:T(8,128)S(1)}, f32[16,256]{1,0:T(8,128)}, u32[]{:S(2)}) copy-start(f32[16,256]{1,0:T(8,128)} %param.16) | copy-start | bytes 49156
  15.1 14.4 %copy-start.7 = (f32[32]{0:T(128)S(1)}, f32[32]{0:T(128)}, u32[]{:S(2)}) copy-start(f32[32]{0:T(128)} %param.12) | copy-start | bytes 388
  15.1 14.4 %copy-start.5 = (f32[32]{0:T(128)S(1)}, f32[32]{0:T(128)}, u32[]{:S(2)}) copy-start(f32[32]{0:T(128)} %param.14) | copy-start | bytes 388
  15.1 15.3 %copy-start.8 = (f32[32]{0:T(128)S(1)}, f32[32]{0:T(128)}, u32[]{:S(2)}) copy-start(f32[32]{0:T(128)} %param.13) | copy-start | bytes 388
  16.2 272.6 %all-gather.2.cloned.1.call-start = ((), (), s32[]{:S(2)}) async-start(), calls=%async_computation.1 | async-start | bytes 9437184 | tf_op jit(solution)/shard_map/all_gather | solution.py:68
  24.4 66.8 %collective-permute-start = (f32[4,32,8,1,256]{4,2,3,1,0:T(8,128)S(1)}, f32[4,32,8,1,256]{4,2,3,1,0:T(8,128)S(1)}, u32[]{:S(2)}, u32[]{:S(2)}) collective-permute-start(f32[4,32,8,1,256]{4,2,3,1,0:T(8,128)S(1)} %copy.236), channel_id=1, source_target_pairs={{0,8},{8,16},{16,24},{1,9},{9,17},{17,25},{2,10},{10,18},{18,26},{... | collective-permute-start | bytes 3145736 | tf_op jit(solution)/shard_map/ppermute | solution.py:14
  27.9 64.4 %collective-permute-start.1 = (f32[4,32,8,1,256]{4,2,3,1,0:T(8,128)}, f32[4,32,8,1,256]{4,2,3,1,0:T(8,128)}, u32[]{:S(2)}, u32[]{:S(2)}) collective-permute-start(f32[4,32,8,1,256]{4,2,3,1,0:T(8,128)} %copy.238), channel_id=1, source_target_pairs={{8,0},{16,8},{24,16},{9,1},{17,9},{25,17},{10,2},{18,10},{26,18},{... | collective-permute-start | bytes 3145736 | tf_op jit(solution)/shard_map/ppermute | solution.py:17
  143.2 3.4 copy-start.2
  146.5 12.1 %copy-start.3 = (f32[2,32,1,16,256]{4,3,2,1,0:T(8,128)S(1)}, f32[2,32,1,16,256]{4,3,2,1,0:T(8,128)}, u32[]{:S(2)}) copy-start(f32[2,32,1,16,256]{4,3,2,1,0:T(8,128)} %get-tuple-element.21) | copy-start | bytes 3145732
  159.8 8.6 %copy-start.6 = (s32[1024]{0:T(1024)S(1)}, s32[1024]{0:T(1024)}, u32[]{:S(2)}) copy-start(s32[1024]{0:T(1024)} %param.17) | copy-start | bytes 12292
  165.0 381.7 %all-reduce.6.cloned.1.call-start = ((), (), s32[]{:S(2)}) async-start(), calls=%async_computation.2 | async-start | bytes 262144 | tf_op jit(solution)/shard_map/psum | solution.py:88
  459.6 7.1 %slice-start = ((s8[8388608]{0:T(1024)(128)(4,1)}), s8[4194304]{0:T(1024)(128)(4,1)S(1)}, s32[]{:S(2)}) async-start(s8[8388608]{0:T(1024)(128)(4,1)} %bitcast.69), calls=%async_computation.3 | async-start | bytes 8388608
  463.1 3.6 slice-start.1
  466.7 2.2 slice-start.2
  467.0 3.3 slice-start.3
  470.2 78.1 %copy-start.1 = (f32[3,32]{1,0:T(4,128)S(1)}, f32[3,32]{1,0:T(4,128)}, u32[]{:S(2)}) copy-start(f32[3,32]{1,0:T(4,128)} %param.11) | copy-start | bytes 1156
Sparse Core Ops, SparseCore 0:
  16.3 73.2 all-reduce.3
  165.2 123.5 all-gather.1
  478.3 68.4 all-reduce.5
where the time goes:
time: 558 us; the launch traced here: 555 us
  waiting for transfers between devices  236 us (42%)
  local copies, waits for them, and re-layouts  216 us (39%)
  other arithmetic  82.2 us (15%)
  between operations  14.8 us (3%)
    all_gather x1, waiting for transfers between devices, per_device(): everything = lax.all_gather(bottom, 'mode', axis=0, tiled=True)  109 us
    scatter x1, local copies, waits for them, and re-layouts, per_device(): bottom.at[:, :, rough_cells]  93.8 us
    psum x1, waiting for transfers between devices, per_device(): lax.psum(jnp.einsum('s,smzxy->zxy', weight_local, fresh), 'mode') / PAIRS  68.6 us
    psum x1, waiting for transfers between devices, per_device(): energy = lax.psum(partial_value, 'mode') / PAIRS  59 us
    sub x1, other arithmetic, per_device(): rhs = field + source[None] - speed * (along + across)  34.3 us
    all_gather x1, local copies, waits for them, and re-layouts, per_device(): everything = lax.all_gather(bottom, 'mode', axis=0, tiled=True)  23.2 us
    gather x3, local copies, waits for them, and re-layouts, per_device(): jnp.take_along_axis(values.transpose(2, 0, 1), targets[:, :, None], axis=1)  21.1 us
    gather x1, local copies, waits for them, and re-layouts, per_device(): values = everything[:, :, rough_cells]  19.9 us
  transfers between devices with their start and end apart: 5, of which 3 were waited for; matrix products, arithmetic and copies ran while one was open for 5% of the time, Pallas kernels for 0%

commit v1 on v0

--- a/solution.py
+++ b/solution.py
@@ -85,7 +85,10 @@
     fresh = jnp.stack([up_new, down_new], axis=1).reshape(
         dirs_local, modes, planes_count, rows, width
     )
-    energy_new = lax.psum(jnp.einsum("s,smzxy->zxy", weight_local, fresh), "mode") / PAIRS
+    energy_new = (
+        jnp.sum(lax.all_gather(jnp.einsum("s,smzxy->zxy", weight_local, fresh), "mode"), axis=0)
+        / PAIRS
+    )
     return (fresh.reshape(pairs_local, planes_count, rows, width), energy_new)
 
 

time: 558 us -> 528 us (0.946)
  waiting for transfers between devices: 236 us -> 206 us
    psum x1 -> x0, waiting for transfers between devices: 68.6 us -> none  [per_device(): lax.psum(jnp.einsum('s,smzxy->zxy', weight_local, fresh), 'mode') / PAIRS]
    all_gather x0 -> x1, waiting for transfers between devices: none -> 38.4 us  [per_device(): lax.all_gather(jnp.einsum('s,smzxy->zxy', weight_local, fresh), 'mode')]
where the time goes in v1:
time: 528 us; the launch traced here: 525 us
  local copies, waits for them, and re-layouts  216 us (41%)
  waiting for transfers between devices  206 us (39%)
  other arithmetic  82.6 us (16%)
  between operations  14.8 us (3%)
    all_gather x1, waiting for transfers between devices, per_device(): everything = lax.all_gather(bottom, 'mode', axis=0, tiled=True)  109 us
    scatter x1, local copies, waits for them, and re-layouts, per_device(): bottom.at[:, :, rough_cells]  93.8 us
    psum x1, waiting for transfers between devices, per_device(): energy = lax.psum(partial_value, 'mode') / PAIRS  59 us
    all_gather x1, waiting for transfers between devices, per_device(): lax.all_gather(jnp.einsum('s,smzxy->zxy', weight_local, fresh), 'mode')  38.4 us
    sub x1, other arithmetic, per_device(): rhs = field + source[None] - speed * (along + across)  34.3 us
    all_gather x1, local copies, waits for them, and re-layouts, per_device(): everything = lax.all_gather(bottom, 'mode', axis=0, tiled=True)  23.2 us
    gather x3, local copies, waits for them, and re-layouts, per_device(): jnp.take_along_axis(values.transpose(2, 0, 1), targets[:, :, None], axis=1)  21.1 us
    gather x1, local copies, waits for them, and re-layouts, per_device(): values = everything[:, :, rough_cells]  19.9 us
  transfers between devices with their start and end apart: 5, of which 3 were waited for; matrix products, arithmetic and copies ran while one was open for 5% of the time, Pallas kernels for 0%

profile of v1, /device:TPU:0, one launch (start us, length us, event | category | flops | bytes accessed | tf_op | source)
XLA Modules:
  0.0 525.0 jit_solution(3384562506161626650)
XLA Ops:
  7.2 7.9 %bitcast_reduce_fusion = bf16[4,8,16,256]{3,2,1,0:T(8,128)(2,1)S(1)} fusion(f32[128,8,16,256]{3,2,1,0:T(8,128)} %param.10), kind=kLoop, calls=%fused_computation.96 | loop fusion | flops 4063232 | bytes 17039360 | tf_op jit(solution)/shard_map/s,smzxy->zxy/reduce_sum | solution.py:38
  15.2 0.4 fusion.23
  15.5 0.7 copy.266
  16.3 8.0 %fusion.37 = (f32[4,32,8,1,256]{4,3,2,1,0:T(1,128)S(1)}, f32[4,32,8,1,256]{4,3,2,1,0:T(1,128)S(1)}) fusion(f32[4,32,8,16,256]{4,3,2,1,0:T(8,128)} %bitcast.68), kind=kLoop, calls=%fused_computation.99 | loop fusion | bytes 4194304 | tf_op jit(solution)/shard_map/slice | solution.py:15
  24.4 2.5 collective-permute-start
  26.9 1.0 copy.238
  27.9 1.5 collective-permute-start.1
  29.4 0.1 constant_dynamic-slice_fusion
  29.6 0.9 broadcast_multiply_fusion.3
  30.5 0.1 broadcast_multiply_fusion.2
  30.6 59.0 %all-reduce.3.cloned.1.call-done = f32[8,16,256]{2,1,0:T(8,128)} async-done(((f32[8,16,256]{2,1,0:T(8,128)}), f32[8,16,256]{2,1,0:T(8,128)}) %all-reduce.3.cloned.1.call-update) | async-done | bytes 131088 | tf_op jit(solution)/shard_map/psum | solution.py:39
  89.6 0.9 add_divide_fusion.8
  90.5 0.6 broadcast_multiply_fusion.1
  91.2 1.1 copy.237
  92.3 2.3 copy.239
  94.6 34.3 %fusion.5 = f32[4,32,8,16,256]{4,3,2,1,0:T(8,128)} fusion(f32[4,32,8,16,256]{4,3,2,1,0:T(8,128)} %bitcast.69, f32[4,32,8,1,256]{4,3,2,1,0:T(1,128)S(1)} %copy.239, f32[4,32,8,1,256]{4,3,2,1,0:T(1,128)S(1)} %copy.237, f32[4]{0:T(128)S(1)} %get-tuple-element.31, f32[4]{0:T(128)S(1)} %get-tuple-element.33, f32[4]{0:T(128)S(1)} %get-tuple-element.30, ...), kind=kLoop, calls=%fused_computation.11 | loop fusion | flops 67108864 | bytes 39846080 | tf_op jit(solution)/shard_map/sub | solution.py:53
  128.9 9.2 %fusion.36 = (f32[2,32,8,16,256]{4,3,2,1,0:T(8,128)}, f32[2,32,8,16,256]{4,3,2,1,0:T(8,128)S(1)}) fusion(f32[4,32,8,16,256]{4,3,2,1,0:T(8,128)} %fusion.5), kind=kLoop, calls=%fused_computation.98 | loop fusion | bytes 33554432 | tf_op jit(solution)/shard_map/slice | solution.py:79
  138.1 1.1 divide_dynamic-update-slice_fusion
  139.2 0.2 constant_dynamic-update-slice_fusion.12
  139.5 0.2 constant_dynamic-update-slice_fusion.10
  139.8 0.2 constant_dynamic-update-slice_fusion.8
  140.1 3.0 fusion.38
  143.2 3.4 copy-done.2
  146.6 2.5 squeeze.36
  149.0 2.4 squeeze.37
  151.4 2.4 squeeze.38
  153.8 2.4 squeeze.39
  156.2 2.4 squeeze.40
  158.6 1.1 squeeze.41
  159.8 0.2 squeeze.42
  160.0 0.2 squeeze.43
  160.2 4.9 add_divide_fusion.7
  165.0 0.3 all-gather.6.cloned.1.call-start
  165.3 0.8 bitcast_or_fusion
  166.1 0.2 copy.242
  166.3 0.3 reshape.137
  166.6 0.8 and_bitcast_fusion
  167.4 0.3 copy.240
  168.4 5.9 %copy.244 = f32[2,32,4096]{1,0,2:T(2,128)} copy(f32[2,32,4096]{2,1,0:T(8,128)} %add_divide_fusion.7) | data formatting | bytes 2097152 | tf_op jit(solution)/shard_map/div | solution.py:62
  174.3 5.7 %gather_fusion.1 = f32[1024,2,32]{2,1,0:T(2,128)S(1)} fusion(f32[2,32,4096]{1,0,2:T(2,128)} %copy.244, s32[1024]{0:T(1024)S(1)} %get-tuple-element.27), kind=kCustom, calls=%fused_computation.1 | custom fusion | bytes 528384 | tf_op jit(solution)/shard_map/gather | solution.py:74
  180.0 108.7 %all-gather.4.cloned.1.call-done = f32[16,32,4096]{2,1,0:T(8,128)} async-done(((f32[2,32,4096]{2,1,0:T(8,128)}), f32[16,32,4096]{2,1,0:T(8,128)}) %all-gather.4.cloned.1.call-update) | async-done | bytes 8388624 | tf_op jit(solution)/shard_map/all_gather | solution.py:68
  288.8 23.2 %copy.241 = f32[16,32,4096]{1,0,2:T(8,128)} copy(f32[16,32,4096]{2,1,0:T(8,128)} %all-gather.4.cloned.1.call-done) | data formatting | bytes 16777216 | tf_op jit(solution)/shard_map/all_gather | solution.py:68
  312.0 19.9 %gather_fusion = f32[1024,16,32]{2,1,0:T(8,128)} fusion(f32[16,32,4096]{1,0,2:T(8,128)} %copy.241, s32[1024]{0:T(1024)S(1)} %get-tuple-element.27), kind=kCustom, calls=%fused_computation | custom fusion | bytes 4198400 | tf_op jit(solution)/shard_map/gather | solution.py:69
  331.9 20.6 %gather_fusion.2 = f32[2048,32]{1,0:T(8,128)S(1)} fusion(f32[1024,16,32]{2,1,0:T(8,128)} %gather_fusion, s32[2048]{0:T(1024)S(1)} %reshape.137), kind=kCustom, calls=%fused_computation.2 | custom fusion | bytes 540672 | tf_op jit(solution)/shard_map/jit(take_along_axis)/gather | solution.py:71
  352.5 3.9 fusion.22
  356.4 93.8 %scatter_fusion = f32[2,32,4096]{1,0,2:T(2,128)} fusion(f32[2,32,4096]{1,0,2:T(2,128)} %copy.244, s32[1024]{0:T(1024)S(1)} %get-tuple-element.28, f32[1024,2,32]{2,1,0:T(2,128)S(1)} %fusion.22), kind=kCustom, calls=%fused_computation.3 | custom fusion | bytes 790528 | tf_op jit(solution)/shard_map/scatter | solution.py:75
  450.2 5.8 %broadcast_multiply_fusion = f32[2,32,4096]{1,0,2:T(2,128)} fusion(f32[2,32,4096]{1,0,2:T(2,128)} %scatter_fusion), kind=kLoop, calls=%fused_computation.22 | loop fusion | flops 262144 | bytes 2097152 | tf_op jit(solution)/shard_map/mul | solution.py:75
  456.0 3.6 copy.254
  459.6 1.6 constant_dynamic-update-slice_fusion.6
  461.3 1.9 constant_dynamic-update-slice_fusion.5
  463.2 1.6 constant_dynamic-update-slice_fusion.4
  464.8 1.9 constant_dynamic-update-slice_fusion.3
  466.7 0.2 constant_dynamic-update-slice_fusion.2
  467.0 0.3 constant_dynamic-update-slice_fusion.1
  467.3 0.2 constant_dynamic-update-slice_fusion
  467.5 0.3 fusion.14
  467.8 1.1 slice-done.2
  468.9 1.3 slice-done.3
  470.2 6.9 %fusion.32 = (bf16[2,2,8,16,256]{4,3,2,1,0:T(8,128)(2,1)S(1)}, f32[2,2,32,8,16,256]{5,4,3,2,1,0:T(8,128)}) fusion(f32[2,1,32,8,16,256]{5,4,3,2,1,0:T(8,128)S(1)} %bitcast.77, f32[2,1,32,8,16,256]{5,4,3,2,1,0:T(8,128)S(1)} %bitcast.74), kind=kLoop, calls=%fused_computation.97 | loop fusion | flops 8257536 | bytes 33816576 | tf_op jit(solution)/shard_map/s,smzxy->zxy/reduce_sum | solution.py:89
  477.1 0.4 fusion.25
  477.5 0.7 copy.265
  478.1 38.4 %all-gather.6.cloned.1.call-done = f32[64,16,256]{2,1,0:T(8,128)} async-done(((f32[8,16,256]{2,1,0:T(8,128)}), f32[64,16,256]{2,1,0:T(8,128)}) %all-gather.6.cloned.1.call-update) | async-done | bytes 1048592 | tf_op jit(solution)/shard_map/all_gather | solution.py:89
  516.5 1.3 reduce_sum.32
  517.8 0.7 broadcast_multiply_fusion.4
  (47 shorter events, 0.6 us)
Async XLA Ops:
  7.2 22.2 %copy-start = (f32[3,32]{1,0:T(4,128)S(1)}, f32[3,32]{1,0:T(4,128)}, u32[]{:S(2)}) copy-start(f32[3,32]{1,0:T(4,128)} %param.11) | copy-start | bytes 1156
  7.2 82.4 %all-reduce.3.cloned.1.call-start = ((), (), s32[]{:S(2)}) async-start(), calls=%async_computation | async-start | bytes 262144 | tf_op jit(solution)/shard_map/psum | solution.py:39
  7.2 7.9 %copy-start.9 = (f32[32]{0:T(128)S(1)}, f32[32]{0:T(128)}, u32[]{:S(2)}) copy-start(f32[32]{0:T(128)} %param.15) | copy-start | bytes 388
  15.1 14.4 %copy-start.4 = (f32[16,256]{1,0:T(8,128)S(1)}, f32[16,256]{1,0:T(8,128)}, u32[]{:S(2)}) copy-start(f32[16,256]{1,0:T(8,128)} %param.16) | copy-start | bytes 49156
  15.1 14.4 %copy-start.7 = (f32[32]{0:T(128)S(1)}, f32[32]{0:T(128)}, u32[]{:S(2)}) copy-start(f32[32]{0:T(128)} %param.12) | copy-start | bytes 388
  15.1 14.4 %copy-start.5 = (f32[32]{0:T(128)S(1)}, f32[32]{0:T(128)}, u32[]{:S(2)}) copy-start(f32[32]{0:T(128)} %param.14) | copy-start | bytes 388
  15.1 15.3 %copy-start.8 = (f32[32]{0:T(128)S(1)}, f32[32]{0:T(128)}, u32[]{:S(2)}) copy-start(f32[32]{0:T(128)} %param.13) | copy-start | bytes 388
  16.2 272.6 %all-gather.4.cloned.1.call-start = ((), (), s32[]{:S(2)}) async-start(), calls=%async_computation.1 | async-start | bytes 9437184 | tf_op jit(solution)/shard_map/all_gather | solution.py:68
  24.4 66.8 %collective-permute-start = (f32[4,32,8,1,256]{4,2,3,1,0:T(8,128)S(1)}, f32[4,32,8,1,256]{4,2,3,1,0:T(8,128)S(1)}, u32[]{:S(2)}, u32[]{:S(2)}) collective-permute-start(f32[4,32,8,1,256]{4,2,3,1,0:T(8,128)S(1)} %copy.236), channel_id=1, source_target_pairs={{0,8},{8,16},{16,24},{1,9},{9,17},{17,25},{2,10},{10,18},{18,26},{... | collective-permute-start | bytes 3145736 | tf_op jit(solution)/shard_map/ppermute | solution.py:14
  27.9 64.4 %collective-permute-start.1 = (f32[4,32,8,1,256]{4,2,3,1,0:T(8,128)}, f32[4,32,8,1,256]{4,2,3,1,0:T(8,128)}, u32[]{:S(2)}, u32[]{:S(2)}) collective-permute-start(f32[4,32,8,1,256]{4,2,3,1,0:T(8,128)} %copy.238), channel_id=1, source_target_pairs={{8,0},{16,8},{24,16},{9,1},{17,9},{25,17},{10,2},{18,10},{26,18},{... | collective-permute-start | bytes 3145736 | tf_op jit(solution)/shard_map/ppermute | solution.py:17
  143.2 3.4 copy-start.2
  146.5 12.1 %copy-start.3 = (f32[2,32,1,16,256]{4,3,2,1,0:T(8,128)S(1)}, f32[2,32,1,16,256]{4,3,2,1,0:T(8,128)}, u32[]{:S(2)}) copy-start(f32[2,32,1,16,256]{4,3,2,1,0:T(8,128)} %get-tuple-element.21) | copy-start | bytes 3145732
  159.8 8.6 %copy-start.6 = (s32[1024]{0:T(1024)S(1)}, s32[1024]{0:T(1024)}, u32[]{:S(2)}) copy-start(s32[1024]{0:T(1024)} %param.17) | copy-start | bytes 12292
  165.0 351.5 %all-gather.6.cloned.1.call-start = ((), (), s32[]{:S(2)}) async-start(), calls=%async_computation.2 | async-start | bytes 1179648 | tf_op jit(solution)/shard_map/all_gather | solution.py:89
  459.6 7.1 %slice-start = ((s8[8388608]{0:T(1024)(128)(4,1)}), s8[4194304]{0:T(1024)(128)(4,1)S(1)}, s32[]{:S(2)}) async-start(s8[8388608]{0:T(1024)(128)(4,1)} %bitcast.70), calls=%async_computation.3 | async-start | bytes 8388608
  463.1 3.6 slice-start.1
  466.7 2.2 slice-start.2
  467.0 3.3 slice-start.3
  470.2 48.3 %copy-start.1 = (f32[3,32]{1,0:T(4,128)S(1)}, f32[3,32]{1,0:T(4,128)}, u32[]{:S(2)}) copy-start(f32[3,32]{1,0:T(4,128)} %param.11) | copy-start | bytes 1156
Sparse Core Ops, SparseCore 0:
  16.3 73.2 all-reduce.2
  165.2 123.5 all-gather.3
  478.3 38.2 all-gather.5
